TPU v7x, 32 devices: a whole 2x2x4 slice. The times are simulated.
32 devices in a mesh: particle: 2 (over x), coil: 8 (over z, y), phase: 2 (over core).
Axes of the slice: x: 2, y: 2, z: 4, core: 2. Of those that a mesh axis runs over, the one named last changes fastest.
Arguments:
- position: float32 [256, 16, 4, 384], P('coil', 'phase', 'particle'), parts along dimension 2, may hold values from -6 to 6
- coil_maps: bfloat16 [8, 256, 4, 384], P('coil', None, 'particle'), parts along dimension 2, may hold values from -2 to 2
- kspace_data: bfloat16 [8, 256, 16, 4, 384], P('coil', None, 'phase', 'particle'), parts along dimension 3, may hold values from -1.796875 to 1.796875
- sample_mask: int32 [256, 16], P(None, 'phase'), may hold values 0 or 1
Outputs:
- gradient: float32 [256, 16, 4, 384], P('coil', 'phase', 'particle'), parts along dimension 2
There are 2 independent parts, one for each index of `particle`. A program takes and returns all parts, laid end to end along the dimension named above; an argument that names none is the same for every part. Nothing has to cross between parts.
All inputs are finite; a program needn't handle non-finite values. No bound on the sum of `sample_mask` on one device may be relied on, other than what follows from the above.
Results may differ from a plain program's by a relative error of at most 0.0012.
Values may be sent and summed in bfloat16 or wider, within the bound.
A program may use at most 64 MiB of HBM per device.

v0:
```python
import math

import jax
import jax.numpy as jnp
from jax import lax
from jax.sharding import PartitionSpec as P


def with_halo(block, sides, width):
    for axis, dim in sides:
        count = lax.axis_size(axis)
        forward = [(i, i + 1) for i in range(count - 1)]
        forward.append((count - 1, 0))
        backward = [(target, source) for source, target in forward]
        low = lax.ppermute(
            lax.slice_in_dim(block, block.shape[dim] - width, None, axis=dim), axis, forward
        )
        high = lax.ppermute(lax.slice_in_dim(block, 0, width, axis=dim), axis, backward)
        block = jnp.concatenate([low, block, high], axis=dim)
    return block


def dft_tables(length):
    counter = jnp.arange(length, dtype=jnp.int32)
    product = counter[:, None] * counter[None, :] % length
    angles = product.astype(jnp.float32) * (2.0 * math.pi / length)
    scaling = 1.0 / math.sqrt(length)
    return (jnp.cos(angles) * scaling, -jnp.sin(angles) * scaling)


def build_tables(rows_total, width):
    row_real, row_imag = dft_tables(rows_total)
    col_real, col_imag = dft_tables(width)
    forward_wide = jnp.concatenate(
        [jnp.concatenate([col_real, col_imag], 1), jnp.concatenate([-col_imag, col_real], 1)], 0
    )
    backward_wide = jnp.concatenate(
        [jnp.concatenate([col_real, -col_imag], 1), jnp.concatenate([col_imag, col_real], 1)], 0
    )
    return (
        row_real.astype(jnp.bfloat16),
        row_imag.astype(jnp.bfloat16),
        forward_wide.astype(jnp.bfloat16),
        backward_wide.astype(jnp.bfloat16),
    )


def complex_times(factor, values, conjugate):
    width = values.shape[-1] // 2
    factor_real = factor[..., :width]
    factor_imag = factor[..., width:]
    if conjugate:
        factor_imag = -factor_imag
    value_real = values[..., :width]
    value_imag = values[..., width:]
    out_real = factor_real * value_real - factor_imag * value_imag
    out_imag = factor_real * value_imag + factor_imag * value_real
    return jnp.concatenate([out_real, out_imag], -1)


def rows_apply(table_real, table_imag, values, adjoint):
    width = values.shape[-1] // 2
    real_part = jnp.einsum("kn,npsd->kpsd", table_real, values, preferred_element_type=jnp.float32)
    imag_part = jnp.einsum("kn,npsd->kpsd", table_imag, values, preferred_element_type=jnp.float32)
    if adjoint:
        out_real = real_part[..., :width] + imag_part[..., width:]
        out_imag = real_part[..., width:] - imag_part[..., :width]
    else:
        out_real = real_part[..., :width] - imag_part[..., width:]
        out_imag = real_part[..., width:] + imag_part[..., :width]
    return jnp.concatenate([out_real, out_imag], -1)


def local(position, coil_maps, kspace_data, sample_mask):
    rows_here = position.shape[0]
    rows_total = coil_maps.shape[1]
    width = position.shape[3] // 2
    row_real, row_imag, forward_wide, backward_wide = build_tables(rows_total, width)
    coil_map = coil_maps[0]
    coil_data = kspace_data[0]
    sample_weight = sample_mask.astype(jnp.float32)[:, :, None, None]
    position_low = position.astype(jnp.bfloat16)
    map_rows = coil_map.astype(jnp.float32)[:, None]
    lifted = complex_times(
        map_rows,
        lax.all_gather(position_low, "coil", axis=0, tiled=True).astype(jnp.float32),
        False,
    ).astype(jnp.bfloat16)
    spread = jnp.einsum(
        "npsc,cd->npsd", lifted, forward_wide, preferred_element_type=jnp.float32
    ).astype(jnp.bfloat16)
    kspace = rows_apply(row_real, row_imag, spread, False)
    residual = (sample_weight * (kspace - coil_data.astype(jnp.float32))).astype(jnp.bfloat16)
    back_rows = rows_apply(row_real, row_imag, residual, True).astype(jnp.bfloat16)
    back = jnp.einsum("npsc,cd->npsd", back_rows, backward_wide, preferred_element_type=jnp.float32)
    map_rows = coil_map.astype(jnp.float32)[:, None]
    summed = lax.psum(complex_times(map_rows, back, True), "coil")
    likelihood = lax.dynamic_slice_in_dim(summed, lax.axis_index("coil") * rows_here, rows_here, 0)
    padded = with_halo(position, (("coil", 0), ("phase", 1)), 1)
    phase_part = 2.0 * position - padded[1:-1, :-2] - padded[1:-1, 2:]
    row_part = 2.0 * position - padded[:-2, 1:-1] - padded[2:, 1:-1]
    return 0.6 * likelihood + 0.5 * phase_part + 0.3 * row_part


def solution(mesh):
    in_specs = (
        P("coil", "phase", "particle", None),
        P("coil", None, "particle", None),
        P("coil", None, "phase", "particle", None),
        P(None, "phase"),
    )
    out_specs = P("coil", "phase", "particle", None)
    return jax.shard_map(local, mesh=mesh, in_specs=in_specs, out_specs=out_specs, check_vma=False)
```

profile of v0, /device:TPU:0, one launch (start us, length us, event | category | flops | bytes accessed | tf_op | source)
XLA Modules:
  0.0 335.2 jit_solution(8550984614529454720)
XLA Ops:
  6.5 0.0 copy-start.4
  6.5 0.0 all-gather.2.cloned.1.call-start
  6.5 2.1 copy.23
  8.7 0.0 all-gather.2.cloned.1.call-update
  8.7 0.0 all-reduce.2.cloned.1.call-start
  8.8 1.3 bitcast_convert_fusion
  10.0 0.7 negate_bitcast_fusion
  10.8 0.0 copy-start
  10.9 0.0 copy-done.4
  10.9 0.9 copy.9
  11.8 0.8 fusion.44
  12.6 0.8 negate_convert_fusion
  13.4 59.4 %all-gather.2.cloned.1.call-done = bf16[256,8,2,384]{3,0,2,1:T(8,128)(2,1)} async-done(((bf16[32,8,2,384]{3,0,2,1:T(8,128)(2,1)}), bf16[256,8,2,384]{3,0,2,1:T(8,128)(2,1)}) %all-gather.2.cloned.1.call-update) | async-done | bytes 3145744 | tf_op jit(solution)/shard_map/all_gather | solution.py:86
  72.8 2.5 convert_element_type.81
  75.4 0.0 copy-done
  75.4 1.8 subtract_convert_fusion
  77.2 2.3 fusion.12
  79.5 1.9 fusion.49
  81.4 4.6 %fusion.53 = f32[256,8,2,384]{3,0,2,1:T(8,128)} fusion(bf16[256,8,2,384]{3,0,2,1:T(8,128)(2,1)S(1)} %fusion.12), kind=kOutput, calls=%fused_computation.82 | convolution fusion | flops 806354944 | bytes 9437184 | tf_op jit(solution)/shard_map/kn,npsd->kpsd/dot_general | solution.py:63
  85.9 9.2 %slice_subtract_fusion.1 = (f32[256,8,2,192]{3,0,2,1:T(8,128)}, f32[256,8,2,192]{3,0,2,1:T(8,128)}) fusion(f32[256,8,2,384]{3,0,2,1:T(8,128)S(1)} %fusion.49, f32[256,8,2,384]{3,0,2,1:T(8,128)} %fusion.53), kind=kLoop, calls=%fused_computation.9 | loop fusion | flops 1572864 | bytes 18874368 | tf_op jit(solution)/shard_map/sub | solution.py:69
  95.2 5.3 %fusion.1 = bf16[256,8,2,384]{3,0,2,1:T(8,128)(2,1)S(1)} fusion(f32[256,8,2,192]{3,0,2,1:T(8,128)} %get-tuple-element.8, f32[256,8,2,192]{3,0,2,1:T(8,128)} %get-tuple-element.7, bf16[1,256,8,2,384]{4,3,2,1,0:T(2,128)(2,1)} %param.6, f32[256,8]{0,1:T(8,128)S(1)} %convert_element_type.79), kind=kLoop, calls=%fused_computation.2 | loop fusion | flops 7864320 | bytes 12591104 | tf_op jit(solution)/shard_map/convert_element_type | solution.py:93
  100.5 1.9 fusion.47
  102.4 1.9 fusion.51
  104.3 2.6 fusion.3
  106.9 0.0 copy-start.1
  106.9 0.0 copy-start.3
  106.9 2.3 fusion.8
  109.2 0.0 copy-done.1
  109.2 0.0 copy-done.3
  109.3 2.0 multiply_subtract_fusion
  111.3 3.9 %pad_maximum_fusion = f32[256,8,2,384]{3,0,2,1:T(8,128)} fusion(f32[256,8,2,192]{3,0,2,1:T(8,128)S(1)} %get-tuple-element.10, f32[256,8,2,192]{3,0,2,1:T(8,128)S(1)} %get-tuple-element.9), kind=kLoop, calls=%fused_computation.3 | loop fusion | flops 1572864 | bytes 12582912 | tf_op jit(solution)/shard_map/concatenate | solution.py:58
  115.2 0.0 copy-start.2
  115.2 0.0 all-reduce.2.cloned.1.call-update
  115.2 1.1 copy-done.2
  116.4 0.6 collective-permute-start
  117.0 4.2 %collective-permute-start.1 = (f32[1,8,2,384]{3,0,2,1:T(1,128)S(1)}, f32[1,8,2,384]{3,0,2,1:T(1,128)S(1)}, u32[]{:S(2)}, u32[]{:S(2)}) collective-permute-start(f32[1,8,2,384]{3,0,2,1:T(1,128)S(1)} %copy.12), channel_id=1, source_target_pairs={{2,0},{4,2},{6,4},{8,6},{10,8},{12,10},{14,12},{0,14},{3,1},{5,3},... | collective-permute-start | bytes 73736 | tf_op jit(solution)/shard_map/ppermute | solution.py:18
  121.2 0.3 copy.6
  121.5 1.6 collective-permute-done
  123.1 0.0 collective-permute-done.1
  123.1 0.1 collective-permute-start.2
  123.2 0.5 collective-permute-start.3
  123.7 0.8 collective-permute-done.2
  124.5 0.2 collective-permute-done.3
  124.7 200.6 %all-reduce.2.cloned.1.call-done = f32[256,8,2,384]{3,0,2,1:T(8,128)} async-done(((f32[256,8,2,384]{3,0,2,1:T(8,128)}), f32[256,8,2,384]{3,0,2,1:T(8,128)}) %all-reduce.2.cloned.1.call-update) | async-done | bytes 6291472 | tf_op jit(solution)/shard_map/psum | solution.py:97
  325.3 1.6 fusion.17
  326.8 1.5 copy.16
  (7 shorter events, 0.2 us)
Async XLA Ops:
  6.5 4.3 %copy-start.4 = (s32[256,8]{0,1:T(8,128)S(1)}, s32[256,8]{0,1:T(8,128)}, u32[]{:S(2)}) copy-start(s32[256,8]{0,1:T(8,128)} %param.7) | copy-start | bytes 24580
  6.5 66.3 %all-gather.2.cloned.1.call-start = ((), (), s32[]{:S(2)}) async-start(), calls=%async_computation | async-start | bytes 3538944 | tf_op jit(solution)/shard_map/all_gather | solution.py:86
  8.7 316.6 %all-reduce.2.cloned.1.call-start = ((), (), s32[]{:S(2)}) async-start(), calls=%async_computation.1 | async-start | bytes 12582912 | tf_op jit(solution)/shard_map/psum | solution.py:97
  10.8 64.5 %copy-start = (f32[256,2,192]{2,0,1:T(8,128)}, f32[256,2,192]{2,0,1:T(8,128)S(1)}, u32[]{:S(2)}) copy-start(f32[256,2,192]{2,0,1:T(8,128)S(1)} %copy.5) | copy-start | bytes 1179652
  106.9 2.3 copy-start.1
  106.9 2.3 copy-start.3
  115.2 1.1 copy-start.2
  116.4 6.7 %collective-permute-start = (f32[1,8,2,384]{3,0,2,1:T(1,128)S(1)}, f32[1,8,2,384]{3,0,2,1:T(1,128)S(1)}, u32[]{:S(2)}, u32[]{:S(2)}) collective-permute-start(f32[1,8,2,384]{3,0,2,1:T(1,128)S(1)} %copy.11), channel_id=1, source_target_pairs={{0,2},{2,4},{4,6},{6,8},{8,10},{10,12},{12,14},{14,0},{1,3},{3,5},... | collective-permute-start | bytes 73736 | tf_op jit(solution)/shard_map/ppermute | solution.py:15
  117.0 6.1 %collective-permute-start.1 = (f32[1,8,2,384]{3,0,2,1:T(1,128)S(1)}, f32[1,8,2,384]{3,0,2,1:T(1,128)S(1)}, u32[]{:S(2)}, u32[]{:S(2)}) collective-permute-start(f32[1,8,2,384]{3,0,2,1:T(1,128)S(1)} %copy.12), channel_id=1, source_target_pairs={{2,0},{4,2},{6,4},{8,6},{10,8},{12,10},{14,12},{0,14},{3,1},{5,3},... | collective-permute-start | bytes 73736 | tf_op jit(solution)/shard_map/ppermute | solution.py:18
  123.1 1.4 collective-permute-start.2
  123.2 1.5 collective-permute-start.3
Sparse Core Ops, SparseCore 0:
  9.6 63.2 all-gather.1
  115.3 209.8 all-reduce.1
where the time goes:
time: 335 us
  waiting for transfers between devices  263 us (79%)
  other arithmetic  32.7 us (10%)
  matrix products  14.8 us (4%)
  between operations  13.6 us (4%)
  local copies, waits for them, and re-layouts  6.04 us (2%)
  starting transfers between devices  5.44 us (2%)
    psum x1, waiting for transfers between devices, local(): summed = lax.psum(complex_times(map_rows, back, True), 'coil')  201 us
    all_gather x1, waiting for transfers between devices, local(): lax.all_gather(position_low, 'coil', axis=0, tiled=True).astype(jnp.float32)  59.4 us
    sub x1, other arithmetic, rows_apply(): out_real = real_part[..., :width] - imag_part[..., width:]  9.23 us
  transfers between devices with their start and end apart: 6, of which 5 were waited for; matrix products, arithmetic and copies ran while one was open for 1% of the time, Pallas kernels for 0%

commit v1 on v0

v1 whole, which is shorter than its diff:
```python
import functools
import math

import jax
import jax.numpy as jnp
import ml_dtypes
import numpy as np
from jax import lax
from jax.experimental import pallas as pl
from jax.experimental.pallas import tpu as pltpu
from jax.sharding import PartitionSpec as P

MESH = pl.DeviceIdType.MESH
YS = 2


def dft_tables(length):
    counter = np.arange(length, dtype=np.int32)
    product = counter[:, None] * counter[None, :] % length
    angles = product.astype(np.float32) * np.float32(2.0 * math.pi / length)
    scaling = np.float32(1.0 / math.sqrt(length))
    return (np.cos(angles) * scaling, -np.sin(angles) * scaling)


def wide_tables(width):
    col_real, col_imag = dft_tables(width)
    forward = np.block([[col_real, col_imag], [-col_imag, col_real]])
    backward = np.block([[col_real, -col_imag], [col_imag, col_real]])
    return forward.astype(ml_dtypes.bfloat16), backward.astype(ml_dtypes.bfloat16)


def row_tables(rows_total):
    row_real, row_imag = dft_tables(rows_total)
    return row_real.astype(ml_dtypes.bfloat16), row_imag.astype(ml_dtypes.bfloat16)


def kernel(
    zs, phases, rows, width,
    pos_ref, edge_ref, map_ref, data_ref, mask_ref, rf_ref, rb_ref, wf_ref, wb_ref,
    out_ref,
    low, gath, posx, halo_rows, fac_a, fac_b, vv, rr, ysend, yrecv, pown, own, zsend, zrecv,
    agz_s, agz_r, agy_s, agy_r, rsy_s, rsy_r, rsz_s, rsz_r, ph_s, ph_r, hr_s, hr_r,
):
    half = width // 2
    lanes = pos_ref.shape[2]
    slices = lanes // width
    side = zs * rows
    total = YS * side
    coils = zs * YS
    coil = lax.axis_index("coil")
    z = coil // YS
    y = coil % YS
    other_y = 1 - y
    partner = z * YS + other_y
    phase_count = lax.axis_size("phase")
    ph = lax.axis_index("phase")
    ph_next = lax.rem(ph + 1, phase_count)
    ph_prev = lax.rem(ph + phase_count - 1, phase_count)
    c_next = lax.rem(coil + 1, coils)
    c_prev = lax.rem(coil + coils - 1, coils)
    z_to = [lax.rem(z + j, zs) for j in range(1, zs)]

    barrier = pltpu.get_barrier_semaphore()
    peers = [{"coil": t * YS + y} for t in z_to] + [{"coil": partner}]
    peers += [{"coil": c_next}, {"coil": c_prev}, {"phase": ph_next}, {"phase": ph_prev}]
    for peer in peers:
        pl.semaphore_signal(barrier, inc=1, device_id=peer, device_id_type=MESH)

    @pl.loop(0, phases)
    def _(p):
        low[p] = pos_ref[p].astype(jnp.bfloat16)

    @pl.loop(0, phases)
    def _(p):
        gath[p, y, z] = low[p]
        posx[p + 1] = pos_ref[p]

    pl.semaphore_wait(barrier, len(peers))

    def ag_z(p, j):
        return pltpu.make_async_remote_copy(
            src_ref=low.at[p], dst_ref=gath.at[p, y, z],
            send_sem=agz_s.at[p, j], recv_sem=agz_r.at[p, j],
            device_id={"coil": z_to[j] * YS + y}, device_id_type=MESH,
        )

    def ag_y(p):
        return pltpu.make_async_remote_copy(
            src_ref=gath.at[p, y], dst_ref=gath.at[p, y],
            send_sem=agy_s.at[p], recv_sem=agy_r.at[p],
            device_id={"coil": partner}, device_id_type=MESH,
        )

    def rs_y(p):
        return pltpu.make_async_remote_copy(
            src_ref=ysend.at[p], dst_ref=yrecv.at[p],
            send_sem=rsy_s.at[p], recv_sem=rsy_r.at[p],
            device_id={"coil": partner}, device_id_type=MESH,
        )

    def rs_z(p, j):
        return pltpu.make_async_remote_copy(
            src_ref=zsend.at[p, z_to[j]], dst_ref=zrecv.at[p, j],
            send_sem=rsz_s.at[p, j], recv_sem=rsz_r.at[p, j],
            device_id={"coil": z_to[j] * YS + y}, device_id_type=MESH,
        )

    def halo_copies():
        yield pltpu.make_async_remote_copy(
            src_ref=pos_ref.at[phases - 1], dst_ref=posx.at[0],
            send_sem=ph_s.at[0], recv_sem=ph_r.at[0],
            device_id={"phase": ph_next}, device_id_type=MESH,
        )
        yield pltpu.make_async_remote_copy(
            src_ref=pos_ref.at[0], dst_ref=posx.at[phases + 1],
            send_sem=ph_s.at[1], recv_sem=ph_r.at[1],
            device_id={"phase": ph_prev}, device_id_type=MESH,
        )
        yield pltpu.make_async_remote_copy(
            src_ref=edge_ref.at[1], dst_ref=halo_rows.at[0],
            send_sem=hr_s.at[0], recv_sem=hr_r.at[0],
            device_id={"coil": c_next}, device_id_type=MESH,
        )
        yield pltpu.make_async_remote_copy(
            src_ref=edge_ref.at[0], dst_ref=halo_rows.at[1],
            send_sem=hr_s.at[1], recv_sem=hr_r.at[1],
            device_id={"coil": c_prev}, device_id_type=MESH,
        )

    @pl.loop(0, phases)
    def _(p):
        for j in range(zs - 1):
            ag_z(p, j).start()

    for copy in halo_copies():
        copy.start()

    first = lax.broadcasted_iota(jnp.int32, (total, width), 1) < half
    for s in range(slices):
        cols = slice(s * width, (s + 1) * width)
        plain = map_ref[:, cols].astype(jnp.float32)
        turned = pltpu.roll(plain, half, 1)
        fac_a[:, cols] = jnp.where(first, plain, turned)
        fac_b[:, cols] = jnp.where(first, -turned, plain)

    def forward(p):
        for j in range(zs - 1):
            ag_z(p, j).wait_recv()
        ag_y(p).start()

    def compute(p):
        for s in range(slices):
            cols = slice(s * width, (s + 1) * width)
            x = gath[p, :, :, :, cols].reshape(total, width).astype(jnp.float32)
            lifted = fac_a[:, cols] * x + fac_b[:, cols] * pltpu.roll(x, half, 1)
            spread = jnp.dot(
                lifted.astype(jnp.bfloat16), wf_ref[...], preferred_element_type=jnp.float32
            ).astype(jnp.bfloat16)
            vv[:total, cols] = spread[:, :width]
            vv[total:, cols] = spread[:, width:]
        weight = mask_ref[p]
        for s in range(slices):
            cols = slice(s * width, (s + 1) * width)
            kspace = jnp.dot(rf_ref[...], vv[:, cols], preferred_element_type=jnp.float32)
            residual = weight * (kspace - data_ref[p, :, cols].astype(jnp.float32))
            turned = pltpu.roll(residual, half, 1)
            rr[:total, cols] = residual.astype(jnp.bfloat16)
            rr[total:, cols] = jnp.where(first, turned, -turned).astype(jnp.bfloat16)
        for s in range(slices):
            cols = slice(s * width, (s + 1) * width)
            back_rows = jnp.dot(
                rb_ref[...], rr[:, cols], preferred_element_type=jnp.float32
            ).astype(jnp.bfloat16)
            back = jnp.dot(back_rows, wb_ref[...], preferred_element_type=jnp.float32)
            pown[p, :, :, cols] = (
                fac_a[:, cols] * back[:, :width] - fac_b[:, cols] * back[:, width:]
            ).reshape(YS, side, width)
        ysend[p] = pown[p, other_y].astype(jnp.bfloat16)

    def middle(p):
        rs_y(p).wait_recv()
        summed = pown[p, y] + yrecv[p].astype(jnp.float32)
        pown[p, y] = summed
        zsend[p] = summed.astype(jnp.bfloat16).reshape(zs, rows, lanes)
        for j in range(zs - 1):
            rs_z(p, j).start()
        own[p] = pown[p, y, pl.ds(pl.multiple_of(z * rows, rows), rows), :]

    forward(0)

    @pl.loop(0, phases)
    def _(p):
        @pl.when(p + 1 < phases)
        def _():
            forward(p + 1)

        ag_y(p).wait_recv()
        compute(p)
        rs_y(p).start()

        @pl.when(p >= 1)
        def _():
            middle(p - 1)

    middle(phases - 1)

    for copy in halo_copies():
        copy.wait()

    row = lax.broadcasted_iota(jnp.int32, (rows, lanes), 0)

    @pl.loop(0, phases)
    def _(p):
        for j in range(zs - 1):
            rs_z(p, j).wait_recv()
        likelihood = own[p]
        for j in range(zs - 1):
            likelihood = likelihood + zrecv[p, j].astype(jnp.float32)
        here = posx[p + 1]
        phase_part = 2.0 * here - posx[p] - posx[p + 2]
        above = jnp.where(row == 0, halo_rows[0, p], pltpu.roll(here, 1, 0))
        below = jnp.where(row == rows - 1, halo_rows[1, p], pltpu.roll(here, rows - 1, 0))
        row_part = 2.0 * here - above - below
        out_ref[p] = 0.6 * likelihood + 0.5 * phase_part + 0.3 * row_part

    @pl.loop(0, phases)
    def _(p):
        for j in range(zs - 1):
            ag_z(p, j).wait_send()
            rs_z(p, j).wait_send()
        ag_y(p).wait_send()
        rs_y(p).wait_send()


def fused(position, coil_maps, kspace_data, sample_mask):
    rows, phases, slices, width = position.shape
    total = coil_maps.shape[1]
    zs = total // rows // YS
    side = zs * rows
    lanes = slices * width
    order = np.arange(total).reshape(zs, YS, rows).transpose(1, 0, 2).reshape(-1)
    row_real, row_imag = row_tables(total)
    rf = np.concatenate([row_real[:, order], row_imag[:, order]], 1)
    rb = np.concatenate([row_real[order], row_imag[order]], 1)
    forward, backward = wide_tables(width // 2)
    half = width // 2
    wf = np.concatenate([forward, -forward[:, half:], forward[:, :half]], 1)
    wb = np.concatenate([backward, backward[:, half:], backward[:, :half]], 1)

    pos = position.transpose(1, 0, 2, 3).reshape(phases, rows, lanes)
    edges = jnp.stack([position[0], position[-1]]).reshape(2, phases, 1, lanes)
    maps = coil_maps[0].reshape(zs, YS, rows, lanes).transpose(1, 0, 2, 3).reshape(total, lanes)
    data = kspace_data[0].transpose(1, 0, 2, 3).reshape(phases, total, lanes)
    weight = sample_mask.astype(jnp.float32).T[:, :, None]

    vmem = pltpu.VMEM
    bf16, f32 = jnp.bfloat16, jnp.float32
    dma = pltpu.SemaphoreType.DMA
    result = pl.pallas_call(
        functools.partial(kernel, zs, phases, rows, width),
        out_shape=jax.ShapeDtypeStruct((phases, rows, lanes), f32),
        in_specs=[pl.BlockSpec(memory_space=vmem)] * 9,
        out_specs=pl.BlockSpec(memory_space=vmem),
        scratch_shapes=[
            vmem((phases, rows, lanes), bf16),
            vmem((phases, YS, zs, rows, lanes), bf16),
            vmem((phases + 2, rows, lanes), f32),
            vmem((2, phases, 1, lanes), f32),
            vmem((total, lanes), f32),
            vmem((total, lanes), f32),
            vmem((2 * total, lanes), bf16),
            vmem((2 * total, lanes), bf16),
            vmem((phases, side, lanes), bf16),
            vmem((phases, side, lanes), bf16),
            vmem((phases, YS, side, lanes), f32),
            vmem((phases, rows, lanes), f32),
            vmem((phases, zs, rows, lanes), bf16),
            vmem((phases, zs - 1, rows, lanes), bf16),
            dma((phases, zs - 1)), dma((phases, zs - 1)),
            dma((phases,)), dma((phases,)),
            dma((phases,)), dma((phases,)),
            dma((phases, zs - 1)), dma((phases, zs - 1)),
            dma((2,)), dma((2,)), dma((2,)), dma((2,)),
        ],
        compiler_params=pltpu.CompilerParams(
            collective_id=0, has_side_effects=True, vmem_limit_bytes=56 << 20
        ),
    )(pos, edges, maps, data, weight, jnp.asarray(rf), jnp.asarray(rb), jnp.asarray(wf), jnp.asarray(wb))
    return result.reshape(phases, rows, slices, width).transpose(1, 0, 2, 3)


def with_halo(block, sides, width):
    for axis, dim in sides:
        count = lax.axis_size(axis)
        forward = [(i, i + 1) for i in range(count - 1)]
        forward.append((count - 1, 0))
        backward = [(target, source) for source, target in forward]
        low = lax.ppermute(
            lax.slice_in_dim(block, block.shape[dim] - width, None, axis=dim), axis, forward
        )
        high = lax.ppermute(lax.slice_in_dim(block, 0, width, axis=dim), axis, backward)
        block = jnp.concatenate([low, block, high], axis=dim)
    return block


def complex_times(factor, values, conjugate):
    width = values.shape[-1] // 2
    factor_real = factor[..., :width]
    factor_imag = factor[..., width:]
    if conjugate:
        factor_imag = -factor_imag
    value_real = values[..., :width]
    value_imag = values[..., width:]
    out_real = factor_real * value_real - factor_imag * value_imag
    out_imag = factor_real * value_imag + factor_imag * value_real
    return jnp.concatenate([out_real, out_imag], -1)


def rows_apply(table_real, table_imag, values, adjoint):
    width = values.shape[-1] // 2
    real_part = jnp.einsum("kn,npsd->kpsd", table_real, values, preferred_element_type=jnp.float32)
    imag_part = jnp.einsum("kn,npsd->kpsd", table_imag, values, preferred_element_type=jnp.float32)
    if adjoint:
        out_real = real_part[..., :width] + imag_part[..., width:]
        out_imag = real_part[..., width:] - imag_part[..., :width]
    else:
        out_real = real_part[..., :width] - imag_part[..., width:]
        out_imag = real_part[..., width:] + imag_part[..., :width]
    return jnp.concatenate([out_real, out_imag], -1)


def general(position, coil_maps, kspace_data, sample_mask):
    rows_total = coil_maps.shape[1]
    width = position.shape[3] // 2
    row_real, row_imag = (jnp.asarray(t) for t in row_tables(rows_total))
    forward_wide, backward_wide = (jnp.asarray(t) for t in wide_tables(width))
    coil_data = kspace_data[0]
    sample_weight = sample_mask.astype(jnp.float32)[:, :, None, None]
    position_low = position.astype(jnp.bfloat16)
    map_rows = coil_maps[0].astype(jnp.float32)[:, None]
    image = lax.all_gather(position_low, "coil", axis=0, tiled=True)
    lifted = complex_times(map_rows, image.astype(jnp.float32), False).astype(jnp.bfloat16)
    spread = jnp.einsum(
        "npsc,cd->npsd", lifted, forward_wide, preferred_element_type=jnp.float32
    ).astype(jnp.bfloat16)
    kspace = rows_apply(row_real, row_imag, spread, False)
    residual = (sample_weight * (kspace - coil_data.astype(jnp.float32))).astype(jnp.bfloat16)
    back_rows = rows_apply(row_real, row_imag, residual, True).astype(jnp.bfloat16)
    back = jnp.einsum("npsc,cd->npsd", back_rows, backward_wide, preferred_element_type=jnp.float32)
    likelihood = lax.psum_scatter(
        complex_times(map_rows, back, True), "coil", scatter_dimension=0, tiled=True
    )
    padded = with_halo(position, (("coil", 0), ("phase", 1)), 1)
    phase_part = 2.0 * position - padded[1:-1, :-2] - padded[1:-1, 2:]
    row_part = 2.0 * position - padded[:-2, 1:-1] - padded[2:, 1:-1]
    return 0.6 * likelihood + 0.5 * phase_part + 0.3 * row_part


def local(position, coil_maps, kspace_data, sample_mask):
    rows = position.shape[0]
    coils = lax.axis_size("coil")
    if coils == 8 and rows % 16 == 0 and position.shape[3] % 128 == 0:
        return fused(position, coil_maps, kspace_data, sample_mask)
    return general(position, coil_maps, kspace_data, sample_mask)


def solution(mesh):
    in_specs = (
        P("coil", "phase", "particle", None),
        P("coil", None, "particle", None),
        P("coil", None, "phase", "particle", None),
        P(None, "phase"),
    )
    out_specs = P("coil", "phase", "particle", None)
    return jax.shard_map(local, mesh=mesh, in_specs=in_specs, out_specs=out_specs, check_vma=False)
```

time: 335 us -> 111 us (0.33)
  waiting for transfers between devices: 263 us -> 0 us
  Pallas kernels: 0 us -> 92.3 us
  other arithmetic: 32.7 us -> 0.03 us
  matrix products: 14.8 us -> 0 us
  between operations: 13.6 us -> 0.05 us
  local copies, waits for them, and re-layouts: 6.04 us -> 18.5 us
  starting transfers between devices: 5.44 us -> 0 us
    psum x1 -> x0, waiting for transfers between devices: 201 us -> none  [local(): summed = lax.psum(complex_times(map_rows, back, True), 'coil')]
    pallas_call x0 -> x1, Pallas kernels: none -> 92.3 us  [fused(): pl.pallas_call(functools.partial(kernel, zs, phases, rows, width), out_sh...]
    all_gather x1 -> x0, waiting for transfers between devices: 59.4 us -> none  [local(): lax.all_gather(position_low, 'coil', axis=0, tiled=True).astype(jnp.float32)]
    reshape x0 -> x7, local copies, waits for them, and re-layouts: none -> 15.4 us  [the longest x2 9.07 us: fused(): data = kspace_data[0].transpose(1, 0, 2, 3).reshape(phases, total, lanes)]
    dot_general x6 -> x0, matrix products: 14.8 us -> none  [the longest x2 6.45 us: rows_apply(): jnp.einsum('kn,npsd->kpsd', table_real, values, preferred_element_type=jn...]
    sub x2 -> x0, other arithmetic: 11.2 us -> none  [the longest x1 9.23 us: rows_apply(): out_real = real_part[..., :width] - imag_part[..., width:]]
    convert_element_type x4 -> x0, other arithmetic: 9.14 us -> none  [the longest x1 5.32 us: local(): (sample_weight * (kspace - coil_data.astype(jnp.float32))).astype(jnp.bfl...]
    another operation x4 -> x1, other arithmetic: 6.02 us -> 0.02 us  [fused(): edges = jnp.stack([position[0], position[-1]]).reshape(2, phases, 1, lanes)]
  transfers between devices with their start and end apart: 6 -> 0, of which waited for: 5 -> 0; matrix products, arithmetic and copies ran while one was open for 1% -> 0% of each run, Pallas kernels for 0% -> 0%
where the time goes in v1:
time: 111 us
  Pallas kernels  92.3 us (83%)
  local copies, waits for them, and re-layouts  18.5 us (17%)
    pallas_call x1, Pallas kernels, fused(): pl.pallas_call(functools.partial(kernel, zs, phases, rows, width), out_sh...  92.3 us
    reshape x2, local copies, waits for them, and re-layouts, fused(): data = kspace_data[0].transpose(1, 0, 2, 3).reshape(phases, total, lanes)  9.07 us
    reshape x2, local copies, waits for them, and re-layouts, fused(): pos = position.transpose(1, 0, 2, 3).reshape(phases, rows, lanes)  2.93 us
    reshape x2, local copies, waits for them, and re-layouts, fused(): return result.reshape(phases, rows, slices, width).transpose(1, 0, 2, 3)  2.7 us

profile of v1, /device:TPU:0, one launch (start us, length us, event | category | flops | bytes accessed | tf_op | source)
XLA Modules:
  0.0 110.9 jit_solution(7735510564359808680)
XLA Ops:
  0.0 0.8 fusion
  0.8 0.7 reshape.16.edge_ref
  1.5 6.8 %reshape.21 = bf16[8,256,768]{2,0,1:T(8,128)(2,1)S(1)} reshape(bf16[8,256,2,384]{3,2,0,1:T(2,128)(2,1)} %bitcast.18) | data formatting | bytes 6291456 | tf_op jit(solution)/shard_map/reshape | solution.py:253
  8.3 2.3 %copy.19.data_ref = bf16[8,256,768]{2,1,0:T(8,128)(2,1)} copy(bf16[8,256,768]{2,0,1:T(8,128)(2,1)S(1)} %reshape.21) | data formatting | bytes 6291456 | tf_op jit(solution)/shard_map/reshape | solution.py:253
  10.6 0.0 copy-start.1
  10.6 0.0 copy-start
  10.6 1.8 %reshape.20 = f32[8,32,768]{2,0,1:T(8,128)S(1)} reshape(f32[8,32,2,384]{3,2,0,1:T(2,128)} %bitcast.20) | data formatting | bytes 1572864 | tf_op jit(solution)/shard_map/reshape | solution.py:250
  12.4 1.1 %copy.18.pos_ref = f32[8,32,768]{2,1,0:T(8,128)} copy(f32[8,32,768]{2,0,1:T(8,128)S(1)} %reshape.20) | data formatting | bytes 1572864 | tf_op jit(solution)/shard_map/reshape | solution.py:250
  13.5 0.0 copy-done.1
  13.5 1.4 %copy.16.mask_ref = f32[8,256,1]{2,1,0:T(8,128)} copy(f32[8,256,1]{1,0,2:T(8,128)S(1)} %convert_bitcast_fusion) | data formatting | bytes 16384 | tf_op jit(solution)/shard_map/broadcast_in_dim | solution.py:254
  14.9 0.0 copy-done
  14.9 0.2 reshape_squeeze.3
  15.1 0.8 copy.14
  15.9 92.3 %shard_map.82 = f32[8,32,768]{2,1,0:T(8,128)} custom-call(f32[8,32,768]{2,1,0:T(8,128)} %copy.18.pos_ref, f32[2,8,1,768]{3,2,1,0:T(1,128)} %reshape.16.edge_ref, bf16[256,768]{1,0:T(8,128)(2,1)} %bitcast.19, bf16[8,256,768]{2,1,0:T(8,128)(2,1)} %copy.19.data_ref, f32[8,256,1]{2,1,0:T(8,128)} %copy.16.mask_ref, bf16[256,512]{1,0:T(8,128)(2,1)} %constant.8.clone.rf_ref, ...), custom_call_target="tpu_custom_call" | custom-call | tf_op jit(solution)/shard_map/pallas_call | solution.py:259
  108.2 1.6 %reshape.19 = f32[8,32,2,384]{3,2,1,0:T(2,128)S(1)} reshape(f32[8,32,768]{2,1,0:T(8,128)} %shard_map.82) | data formatting | bytes 1572864 | tf_op jit(solution)/shard_map/reshape | solution.py:289
  109.8 1.1 %copy.21 = f32[8,32,2,384]{3,2,0,1:T(2,128)} copy(f32[8,32,2,384]{3,2,1,0:T(2,128)S(1)} %reshape.19) | data formatting | bytes 1572864 | tf_op jit(solution)/shard_map/reshape | solution.py:289
  (2 shorter events, 0.0 us)
Async XLA Ops:
  10.6 2.9 %copy-start.1 = (s32[256,8]{0,1:T(8,128)S(1)}, s32[256,8]{0,1:T(8,128)}, u32[]{:S(2)}) copy-start(s32[256,8]{0,1:T(8,128)} %param.11) | copy-start | bytes 24580
  10.6 4.3 %copy-start = (bf16[1,256,2,384]{3,2,1,0:T(2,128)(2,1)S(1)}, bf16[1,256,2,384]{3,2,1,0:T(2,128)(2,1)}, u32[]{:S(2)}) copy-start(bf16[1,256,2,384]{3,2,1,0:T(2,128)(2,1)} %param.9) | copy-start | bytes 1179652

commit v2 on v1

--- a/solution.py
+++ b/solution.py
@@ -36,14 +36,14 @@
 
 def kernel(
     zs, phases, rows, width,
-    pos_ref, edge_ref, map_ref, data_ref, mask_ref, rf_ref, rb_ref, wf_ref, wb_ref,
+    pos_ref, map_ref, data_hbm, mask_ref, rf_ref, rb_ref, wf_ref, wb_ref,
     out_ref,
-    low, gath, posx, halo_rows, fac_a, fac_b, vv, rr, ysend, yrecv, pown, own, zsend, zrecv,
-    agz_s, agz_r, agy_s, agy_r, rsy_s, rsy_r, rsz_s, rsz_r, ph_s, ph_r, hr_s, hr_r,
+    data, edge, mask, low, gath, posx, halo_rows, fac_a, fac_b, vv, rr, ysend, yrecv, pown, own, zsend, zrecv,
+    agz_s, agz_r, agy_s, agy_r, rsy_s, rsy_r, rsz_s, rsz_r, ph_s, ph_r, hr_s, hr_r, data_s,
 ):
     half = width // 2
-    lanes = pos_ref.shape[2]
-    slices = lanes // width
+    slices = pos_ref.shape[2]
+    lanes = slices * width
     side = zs * rows
     total = YS * side
     coils = zs * YS
@@ -66,14 +66,20 @@
     for peer in peers:
         pl.semaphore_signal(barrier, inc=1, device_id=peer, device_id_type=MESH)
 
-    @pl.loop(0, phases)
-    def _(p):
-        low[p] = pos_ref[p].astype(jnp.bfloat16)
-
-    @pl.loop(0, phases)
-    def _(p):
+    def data_copy(p):
+        return pltpu.make_async_copy(data_hbm.at[:, p], data.at[p], data_s.at[p])
+
+    @pl.loop(0, phases)
+    def _(p):
+        data_copy(p).start()
+        for s in range(slices):
+            cols = slice(s * width, (s + 1) * width)
+            posx[p + 1, :, cols] = pos_ref[:, p, s, :]
+        here = posx[p + 1]
+        edge[0, p] = here[:1]
+        edge[1, p] = here[rows - 1:]
+        low[p] = here.astype(jnp.bfloat16)
         gath[p, y, z] = low[p]
-        posx[p + 1] = pos_ref[p]
 
     pl.semaphore_wait(barrier, len(peers))
 
@@ -107,22 +113,22 @@
 
     def halo_copies():
         yield pltpu.make_async_remote_copy(
-            src_ref=pos_ref.at[phases - 1], dst_ref=posx.at[0],
+            src_ref=posx.at[phases], dst_ref=posx.at[0],
             send_sem=ph_s.at[0], recv_sem=ph_r.at[0],
             device_id={"phase": ph_next}, device_id_type=MESH,
         )
         yield pltpu.make_async_remote_copy(
-            src_ref=pos_ref.at[0], dst_ref=posx.at[phases + 1],
+            src_ref=posx.at[1], dst_ref=posx.at[phases + 1],
             send_sem=ph_s.at[1], recv_sem=ph_r.at[1],
             device_id={"phase": ph_prev}, device_id_type=MESH,
         )
         yield pltpu.make_async_remote_copy(
-            src_ref=edge_ref.at[1], dst_ref=halo_rows.at[0],
+            src_ref=edge.at[1], dst_ref=halo_rows.at[0],
             send_sem=hr_s.at[0], recv_sem=hr_r.at[0],
             device_id={"coil": c_next}, device_id_type=MESH,
         )
         yield pltpu.make_async_remote_copy(
-            src_ref=edge_ref.at[0], dst_ref=halo_rows.at[1],
+            src_ref=edge.at[0], dst_ref=halo_rows.at[1],
             send_sem=hr_s.at[1], recv_sem=hr_r.at[1],
             device_id={"coil": c_prev}, device_id_type=MESH,
         )
@@ -138,10 +144,14 @@
     first = lax.broadcasted_iota(jnp.int32, (total, width), 1) < half
     for s in range(slices):
         cols = slice(s * width, (s + 1) * width)
-        plain = map_ref[:, cols].astype(jnp.float32)
+        plain = jnp.concatenate(
+            [map_ref[pl.ds((b % zs * YS + b // zs) * rows, rows), cols] for b in range(coils)], 0
+        ).astype(jnp.float32)
         turned = pltpu.roll(plain, half, 1)
         fac_a[:, cols] = jnp.where(first, plain, turned)
         fac_b[:, cols] = jnp.where(first, -turned, plain)
+
+    mask[...] = mask_ref[...].astype(jnp.float32).T
 
     def forward(p):
         for j in range(zs - 1):
@@ -158,11 +168,13 @@
             ).astype(jnp.bfloat16)
             vv[:total, cols] = spread[:, :width]
             vv[total:, cols] = spread[:, width:]
-        weight = mask_ref[p]
+        lane = lax.broadcasted_iota(jnp.int32, mask.shape, 1)
+        weight = jnp.sum(jnp.where(lane == p, mask[...], 0.0), axis=1, keepdims=True)
+        data_copy(p).wait()
         for s in range(slices):
             cols = slice(s * width, (s + 1) * width)
             kspace = jnp.dot(rf_ref[...], vv[:, cols], preferred_element_type=jnp.float32)
-            residual = weight * (kspace - data_ref[p, :, cols].astype(jnp.float32))
+            residual = weight * (kspace - data[p, :, s, :].astype(jnp.float32))
             turned = pltpu.roll(residual, half, 1)
             rr[:total, cols] = residual.astype(jnp.bfloat16)
             rr[total:, cols] = jnp.where(first, turned, -turned).astype(jnp.bfloat16)
@@ -221,7 +233,9 @@
         above = jnp.where(row == 0, halo_rows[0, p], pltpu.roll(here, 1, 0))
         below = jnp.where(row == rows - 1, halo_rows[1, p], pltpu.roll(here, rows - 1, 0))
         row_part = 2.0 * here - above - below
-        out_ref[p] = 0.6 * likelihood + 0.5 * phase_part + 0.3 * row_part
+        grad = 0.6 * likelihood + 0.5 * phase_part + 0.3 * row_part
+        for s in range(slices):
+            out_ref[:, p, s, :] = grad[:, s * width : (s + 1) * width]
 
     @pl.loop(0, phases)
     def _(p):
@@ -247,21 +261,20 @@
     wf = np.concatenate([forward, -forward[:, half:], forward[:, :half]], 1)
     wb = np.concatenate([backward, backward[:, half:], backward[:, :half]], 1)
 
-    pos = position.transpose(1, 0, 2, 3).reshape(phases, rows, lanes)
-    edges = jnp.stack([position[0], position[-1]]).reshape(2, phases, 1, lanes)
-    maps = coil_maps[0].reshape(zs, YS, rows, lanes).transpose(1, 0, 2, 3).reshape(total, lanes)
-    data = kspace_data[0].transpose(1, 0, 2, 3).reshape(phases, total, lanes)
-    weight = sample_mask.astype(jnp.float32).T[:, :, None]
+    maps = coil_maps[0].reshape(total, lanes)
 
     vmem = pltpu.VMEM
     bf16, f32 = jnp.bfloat16, jnp.float32
     dma = pltpu.SemaphoreType.DMA
-    result = pl.pallas_call(
+    return pl.pallas_call(
         functools.partial(kernel, zs, phases, rows, width),
-        out_shape=jax.ShapeDtypeStruct((phases, rows, lanes), f32),
-        in_specs=[pl.BlockSpec(memory_space=vmem)] * 9,
+        out_shape=jax.ShapeDtypeStruct(position.shape, f32),
+        in_specs=[pl.BlockSpec(memory_space=pl.ANY if i == 2 else vmem) for i in range(8)],
         out_specs=pl.BlockSpec(memory_space=vmem),
         scratch_shapes=[
+            vmem((phases, total, slices, width), bf16),
+            vmem((2, phases, 1, lanes), f32),
+            vmem((total, phases), f32),
             vmem((phases, rows, lanes), bf16),
             vmem((phases, YS, zs, rows, lanes), bf16),
             vmem((phases + 2, rows, lanes), f32),
@@ -280,13 +293,12 @@
             dma((phases,)), dma((phases,)),
             dma((phases,)), dma((phases,)),
             dma((phases, zs - 1)), dma((phases, zs - 1)),
-            dma((2,)), dma((2,)), dma((2,)), dma((2,)),
+            dma((2,)), dma((2,)), dma((2,)), dma((2,)), dma((phases,)),
         ],
         compiler_params=pltpu.CompilerParams(
             collective_id=0, has_side_effects=True, vmem_limit_bytes=56 << 20
         ),
-    )(pos, edges, maps, data, weight, jnp.asarray(rf), jnp.asarray(rb), jnp.asarray(wf), jnp.asarray(wb))
-    return result.reshape(phases, rows, slices, width).transpose(1, 0, 2, 3)
+    )(position, maps, kspace_data[0], sample_mask.T, jnp.asarray(rf), jnp.asarray(rb), jnp.asarray(wf), jnp.asarray(wb))
 
 
 def with_halo(block, sides, width):

time: 111 us -> 95.7 us (0.86)
  local copies, waits for them, and re-layouts: 18.5 us -> 4.07 us
    reshape x7 -> x0, local copies, waits for them, and re-layouts: 15.4 us -> none  [the longest x2 9.07 us: fused(): data = kspace_data[0].transpose(1, 0, 2, 3).reshape(phases, total, lanes)]
    unnamed x4 -> x2, local copies, waits for them, and re-layouts: 0.01 us -> 4.07 us
    broadcast_in_dim x1 -> x0, local copies, waits for them, and re-layouts: 1.35 us -> none  [fused(): weight = sample_mask.astype(jnp.float32).T[:, :, None]]
where the time goes in v2:
time: 95.7 us; the launch traced here: 95.4 us
  Pallas kernels  91.4 us (96%)
  local copies, waits for them, and re-layouts  4.07 us (4%)
    pallas_call x1, Pallas kernels, fused(): pl.pallas_call(functools.partial(kernel, zs, phases, rows, width), out_sh...  91.4 us
    unnamed x2, local copies, waits for them, and re-layouts  4.07 us

profile of v2, /device:TPU:0, one launch (start us, length us, event | category | flops | bytes accessed | tf_op | source)
XLA Modules:
  0.0 95.4 jit_solution(16311720439665646850)
XLA Ops:
  0.0 1.8 %copy.9 = bf16[32,8,2,384]{3,1,2,0:T(8,128)(2,1)} copy(bf16[32,8,2,384]{3,2,1,0:T(2,128)(2,1)} %bitcast.7) | data formatting | bytes 786432
  1.8 91.4 %shard_map.82 = f32[32,8,2,384]{3,2,1,0:T(2,128)} custom-call(f32[32,8,2,384]{3,2,1,0:T(2,128)} %pos_ref.1, bf16[256,768]{1,0:T(8,128)(2,1)} %bitcast.6, bf16[256,8,2,384]{3,2,1,0:T(2,128)(2,1)} %bitcast.5, s32[8,256]{1,0:T(8,128)} %bitcast.8, bf16[256,512]{1,0:T(8,128)(2,1)} %constant.8.clone.rf_ref, bf16[256,512]{1,0:T(8,128)(2,1)} %constant.9.clone.rb_ref, ...), custom_call_target="tpu_custom_call" | custom-call | tf_op jit(solution)/shard_map/pallas_call | solution.py:269
  93.2 2.3 %copy.11 = f32[32,8,2,384]{3,2,1,0:T(2,128)} copy(f32[32,8,2,384]{3,2,1,0:T(2,128)} %shard_map.82) | data formatting | bytes 1572864

commit v3 on v2

--- a/solution.py
+++ b/solution.py
@@ -38,8 +38,8 @@
     zs, phases, rows, width,
     pos_ref, map_ref, data_hbm, mask_ref, rf_ref, rb_ref, wf_ref, wb_ref,
     out_ref,
-    data, edge, mask, low, gath, posx, halo_rows, fac_a, fac_b, vv, rr, ysend, yrecv, pown, own, zsend, zrecv,
-    agz_s, agz_r, agy_s, agy_r, rsy_s, rsy_r, rsz_s, rsz_r, ph_s, ph_r, hr_s, hr_r, data_s,
+    data, edge, mask, low, gath, posx, halo_rows, fac_a, fac_b, vv, rr, ysend, yrecv, pown, own, zsend, zmid, zrecv,
+    agz_s, agz_r, agy_s, agy_r, rsy_s, rsy_r, rsz_s, rsz_r, rsm_s, rsm_r, ph_s, ph_r, hr_s, hr_r, data_s,
 ):
     half = width // 2
     slices = pos_ref.shape[2]
@@ -60,6 +60,20 @@
     c_prev = lax.rem(coil + coils - 1, coils)
     z_to = [lax.rem(z + j, zs) for j in range(1, zs)]
 
+    away = z // 2
+    inner = (z == 1) | (z == 2)
+    outer = (z == 0) | (z == 3)
+    mate = away * 2 + 1 - z % 2
+    facing = 2 - away
+    opp = (1 - away) * 2
+    columns = (y, other_y)
+
+    def swapped(p):
+        return p % 4 == 2
+
+    def straight(p):
+        return p % 4 != 2
+
     barrier = pltpu.get_barrier_semaphore()
     peers = [{"coil": t * YS + y} for t in z_to] + [{"coil": partner}]
     peers += [{"coil": c_next}, {"coil": c_prev}, {"phase": ph_next}, {"phase": ph_prev}]
@@ -83,12 +97,25 @@
 
     pl.semaphore_wait(barrier, len(peers))
 
-    def ag_z(p, j):
-        return pltpu.make_async_remote_copy(
-            src_ref=low.at[p], dst_ref=gath.at[p, y, z],
-            send_sem=agz_s.at[p, j], recv_sem=agz_r.at[p, j],
-            device_id={"coil": z_to[j] * YS + y}, device_id_type=MESH,
-        )
+    def ag_z(p, col, src, to, slot):
+        return pltpu.make_async_remote_copy(
+            src_ref=gath.at[p, col, src], dst_ref=gath.at[p, col, src],
+            send_sem=agz_s.at[p, col, slot], recv_sem=agz_r.at[p, col, src],
+            device_id={"coil": to * YS + y}, device_id_type=MESH,
+        )
+
+    def ag_own(p, col):
+        return [ag_z(p, col, z, mate, 0), ag_z(p, col, z, facing, 1)]
+
+    def ag_relay(p, col):
+        return [ag_z(p, col, opp + k, mate, 2 + k) for k in range(2)]
+
+    def wait_opp(p, col):
+        for k in range(2):
+            ag_z(p, col, opp + k, mate, 2 + k).wait_recv()
+
+    def wait_mate(p, col):
+        ag_z(p, col, mate, mate, 0).wait_recv()
 
     def ag_y(p):
         return pltpu.make_async_remote_copy(
@@ -97,18 +124,46 @@
             device_id={"coil": partner}, device_id_type=MESH,
         )
 
+    def ag_y_one(p):
+        return pltpu.make_async_remote_copy(
+            src_ref=gath.at[p, y, z], dst_ref=gath.at[p, y, z],
+            send_sem=agy_s.at[p], recv_sem=agy_r.at[p],
+            device_id={"coil": partner}, device_id_type=MESH,
+        )
+
+    def rs_y_one(p):
+        return pltpu.make_async_remote_copy(
+            src_ref=ysend.at[p, pl.ds(0, rows)], dst_ref=yrecv.at[p, pl.ds(0, rows)],
+            send_sem=rsy_s.at[p], recv_sem=rsy_r.at[p],
+            device_id={"coil": partner}, device_id_type=MESH,
+        )
+
+    def rs_mate(p, col):
+        return pltpu.make_async_remote_copy(
+            src_ref=zsend.at[p, col, mate], dst_ref=zrecv.at[p, col, 0],
+            send_sem=rsz_s.at[p, col, 0], recv_sem=rsz_r.at[p, col, 0],
+            device_id={"coil": mate * YS + y}, device_id_type=MESH,
+        )
+
+    def rs_mid(p, col):
+        return pltpu.make_async_remote_copy(
+            src_ref=zsend.at[p, col, pl.ds(opp, 2)], dst_ref=zmid.at[p, col],
+            send_sem=rsm_s.at[p, col], recv_sem=rsm_r.at[p, col],
+            device_id={"coil": mate * YS + y}, device_id_type=MESH,
+        )
+
+    def rs_cross(p, col, k):
+        return pltpu.make_async_remote_copy(
+            src_ref=zsend.at[p, col, opp + k], dst_ref=zrecv.at[p, col, 1],
+            send_sem=rsz_s.at[p, col, 1 + k], recv_sem=rsz_r.at[p, col, 1],
+            device_id={"coil": (opp + k) * YS + y}, device_id_type=MESH,
+        )
+
     def rs_y(p):
         return pltpu.make_async_remote_copy(
             src_ref=ysend.at[p], dst_ref=yrecv.at[p],
             send_sem=rsy_s.at[p], recv_sem=rsy_r.at[p],
             device_id={"coil": partner}, device_id_type=MESH,
-        )
-
-    def rs_z(p, j):
-        return pltpu.make_async_remote_copy(
-            src_ref=zsend.at[p, z_to[j]], dst_ref=zrecv.at[p, j],
-            send_sem=rsz_s.at[p, j], recv_sem=rsz_r.at[p, j],
-            device_id={"coil": z_to[j] * YS + y}, device_id_type=MESH,
         )
 
     def halo_copies():
@@ -135,8 +190,12 @@
 
     @pl.loop(0, phases)
     def _(p):
-        for j in range(zs - 1):
-            ag_z(p, j).start()
+        for copy in ag_own(p, y):
+            copy.start()
+
+        @pl.when(swapped(p))
+        def _():
+            ag_y_one(p).start()
 
     for copy in halo_copies():
         copy.start()
@@ -153,10 +212,50 @@
 
     mask[...] = mask_ref[...].astype(jnp.float32).T
 
-    def forward(p):
-        for j in range(zs - 1):
-            ag_z(p, j).wait_recv()
-        ag_y(p).start()
+    def gather_one(p):
+        @pl.when(straight(p) & inner)
+        def _():
+            wait_opp(p, y)
+            for copy in ag_relay(p, y):
+                copy.start()
+
+        @pl.when(swapped(p))
+        def _():
+            ag_y_one(p).wait_recv()
+            for copy in ag_own(p, other_y):
+                copy.start()
+
+    def gather_two(p):
+        @pl.when(straight(p))
+        def _():
+            @pl.when(outer)
+            def _():
+                wait_opp(p, y)
+
+            wait_mate(p, y)
+            ag_y(p).start()
+
+        @pl.when(swapped(p) & inner)
+        def _():
+            for col in columns:
+                wait_opp(p, col)
+                for copy in ag_relay(p, col):
+                    copy.start()
+
+    def gather_end(p):
+        @pl.when(straight(p))
+        def _():
+            ag_y(p).wait_recv()
+
+        @pl.when(swapped(p))
+        def _():
+            @pl.when(outer)
+            def _():
+                for col in columns:
+                    wait_opp(p, col)
+
+            for col in columns:
+                wait_mate(p, col)
 
     def compute(p):
         for s in range(slices):
@@ -187,47 +286,96 @@
             pown[p, :, :, cols] = (
                 fac_a[:, cols] * back[:, :width] - fac_b[:, cols] * back[:, width:]
             ).reshape(YS, side, width)
-        ysend[p] = pown[p, other_y].astype(jnp.bfloat16)
-
-    def middle(p):
-        rs_y(p).wait_recv()
-        summed = pown[p, y] + yrecv[p].astype(jnp.float32)
-        pown[p, y] = summed
-        zsend[p] = summed.astype(jnp.bfloat16).reshape(zs, rows, lanes)
-        for j in range(zs - 1):
-            rs_z(p, j).start()
-        own[p] = pown[p, y, pl.ds(pl.multiple_of(z * rows, rows), rows), :]
-
-    forward(0)
+
+    def send_rows(p, col):
+        zsend[p, col] = pown[p, col].astype(jnp.bfloat16).reshape(zs, rows, lanes)
+        rs_mate(p, col).start()
+
+        @pl.when(outer)
+        def _():
+            rs_mid(p, col).start()
+
+    def cross_rows(p, col):
+        rs_mid(p, col).wait_recv()
+        for k in range(2):
+            at = pl.ds(pl.multiple_of((opp + k) * rows, rows), rows)
+            both = pown[p, col, at, :] + zmid[p, col, k].astype(jnp.float32)
+            zsend[p, col, opp + k] = both.astype(jnp.bfloat16)
+            rs_cross(p, col, k).start()
+
+    def own_rows(p, col):
+        rs_mate(p, col).wait_recv()
+        rs_cross(p, col, 0).wait_recv()
+        mine = pown[p, col, pl.ds(pl.multiple_of(z * rows, rows), rows), :]
+        return mine + zrecv[p, col, 0].astype(jnp.float32) + zrecv[p, col, 1].astype(jnp.float32)
+
+    def reduce_start(p):
+        @pl.when(straight(p))
+        def _():
+            ysend[p] = pown[p, other_y].astype(jnp.bfloat16)
+            rs_y(p).start()
+
+        @pl.when(swapped(p))
+        def _():
+            for col in columns:
+                send_rows(p, col)
+
+    def reduce_one(p):
+        @pl.when(straight(p))
+        def _():
+            rs_y(p).wait_recv()
+            pown[p, y] = pown[p, y] + yrecv[p].astype(jnp.float32)
+            send_rows(p, y)
+
+        @pl.when(swapped(p) & inner)
+        def _():
+            for col in columns:
+                cross_rows(p, col)
+
+    def reduce_two(p):
+        @pl.when(straight(p) & inner)
+        def _():
+            cross_rows(p, y)
+
+        @pl.when(swapped(p))
+        def _():
+            ysend[p, :rows] = own_rows(p, other_y).astype(jnp.bfloat16)
+            rs_y_one(p).start()
+
+    def during(p, step):
+        @pl.when((p >= 0) & (p < phases))
+        def _():
+            step(p)
+
+    @pl.loop(0, phases + 4)
+    def _(t):
+        during(t, gather_one)
+        during(t - 1, gather_two)
+
+        def whole(p):
+            gather_end(p)
+            compute(p)
+            reduce_start(p)
+
+        during(t - 2, whole)
+        during(t - 3, reduce_one)
+        during(t - 4, reduce_two)
+
+    for copy in halo_copies():
+        copy.wait()
+
+    row = lax.broadcasted_iota(jnp.int32, (rows, lanes), 0)
 
     @pl.loop(0, phases)
     def _(p):
-        @pl.when(p + 1 < phases)
-        def _():
-            forward(p + 1)
-
-        ag_y(p).wait_recv()
-        compute(p)
-        rs_y(p).start()
-
-        @pl.when(p >= 1)
-        def _():
-            middle(p - 1)
-
-    middle(phases - 1)
-
-    for copy in halo_copies():
-        copy.wait()
-
-    row = lax.broadcasted_iota(jnp.int32, (rows, lanes), 0)
-
-    @pl.loop(0, phases)
-    def _(p):
-        for j in range(zs - 1):
-            rs_z(p, j).wait_recv()
+        own[p] = own_rows(p, y)
+
+        @pl.when(swapped(p))
+        def _():
+            rs_y_one(p).wait_recv()
+            own[p] = own[p] + yrecv[p, :rows].astype(jnp.float32)
+
         likelihood = own[p]
-        for j in range(zs - 1):
-            likelihood = likelihood + zrecv[p, j].astype(jnp.float32)
         here = posx[p + 1]
         phase_part = 2.0 * here - posx[p] - posx[p + 2]
         above = jnp.where(row == 0, halo_rows[0, p], pltpu.roll(here, 1, 0))
@@ -239,11 +387,34 @@
 
     @pl.loop(0, phases)
     def _(p):
-        for j in range(zs - 1):
-            ag_z(p, j).wait_send()
-            rs_z(p, j).wait_send()
-        ag_y(p).wait_send()
-        rs_y(p).wait_send()
+        def column_sent(col):
+            for copy in ag_own(p, col):
+                copy.wait_send()
+            rs_mate(p, col).wait_send()
+
+            @pl.when(inner)
+            def _():
+                for k in range(2):
+                    rs_cross(p, col, k).wait_send()
+                for copy in ag_relay(p, col):
+                    copy.wait_send()
+
+            @pl.when(outer)
+            def _():
+                rs_mid(p, col).wait_send()
+
+        column_sent(y)
+
+        @pl.when(straight(p))
+        def _():
+            ag_y(p).wait_send()
+            rs_y(p).wait_send()
+
+        @pl.when(swapped(p))
+        def _():
+            column_sent(other_y)
+            ag_y_one(p).wait_send()
+            rs_y_one(p).wait_send()
 
 
 def fused(position, coil_maps, kspace_data, sample_mask):
@@ -287,12 +458,14 @@
             vmem((phases, side, lanes), bf16),
             vmem((phases, YS, side, lanes), f32),
             vmem((phases, rows, lanes), f32),
-            vmem((phases, zs, rows, lanes), bf16),
-            vmem((phases, zs - 1, rows, lanes), bf16),
-            dma((phases, zs - 1)), dma((phases, zs - 1)),
+            vmem((phases, YS, zs, rows, lanes), bf16),
+            vmem((phases, YS, 2, rows, lanes), bf16),
+            vmem((phases, YS, 2, rows, lanes), bf16),
+            dma((phases, YS, 4)), dma((phases, YS, zs)),
             dma((phases,)), dma((phases,)),
             dma((phases,)), dma((phases,)),
-            dma((phases, zs - 1)), dma((phases, zs - 1)),
+            dma((phases, YS, 3)), dma((phases, YS, 2)),
+            dma((phases, YS)), dma((phases, YS)),
             dma((2,)), dma((2,)), dma((2,)), dma((2,)), dma((phases,)),
         ],
         compiler_params=pltpu.CompilerParams(

time: 95.7 us -> 90 us (0.940)
  Pallas kernels: 91.4 us -> 85.7 us
    pallas_call x1, Pallas kernels: 91.4 us -> 85.7 us  [fused(): pl.pallas_call(functools.partial(kernel, zs, phases, rows, width), out_sh...]
where the time goes in v3:
time: 90 us; the launch traced here: 89.8 us
  Pallas kernels  85.7 us (95%)
  local copies, waits for them, and re-layouts  4.07 us (5%)
    pallas_call x1, Pallas kernels, fused(): pl.pallas_call(functools.partial(kernel, zs, phases, rows, width), out_sh...  85.7 us
    unnamed x2, local copies, waits for them, and re-layouts  4.07 us

profile of v3, /device:TPU:0, one launch (start us, length us, event | category | flops | bytes accessed | tf_op | source)
XLA Modules:
  0.0 89.8 jit_solution(15006670656509615427)
XLA Ops:
  0.0 1.8 %copy.9 = bf16[32,8,2,384]{3,1,2,0:T(8,128)(2,1)} copy(bf16[32,8,2,384]{3,2,1,0:T(2,128)(2,1)} %bitcast.7) | data formatting | bytes 786432
  1.8 85.7 %shard_map.82 = f32[32,8,2,384]{3,2,1,0:T(2,128)} custom-call(f32[32,8,2,384]{3,2,1,0:T(2,128)} %pos_ref.1, bf16[256,768]{1,0:T(8,128)(2,1)} %bitcast.6, bf16[256,8,2,384]{3,2,1,0:T(2,128)(2,1)} %bitcast.5, s32[8,256]{1,0:T(8,128)} %bitcast.8, bf16[256,512]{1,0:T(8,128)(2,1)} %constant.8.clone.rf_ref, bf16[256,512]{1,0:T(8,128)(2,1)} %constant.9.clone.rb_ref, ...), custom_call_target="tpu_custom_call" | custom-call | tf_op jit(solution)/shard_map/pallas_call | solution.py:440
  87.5 2.3 %copy.11 = f32[32,8,2,384]{3,2,1,0:T(2,128)} copy(f32[32,8,2,384]{3,2,1,0:T(2,128)} %shard_map.82) | data formatting | bytes 1572864

commit v4 on v3

--- a/solution.py
+++ b/solution.py
@@ -117,17 +117,10 @@
     def wait_mate(p, col):
         ag_z(p, col, mate, mate, 0).wait_recv()
 
-    def ag_y(p):
-        return pltpu.make_async_remote_copy(
-            src_ref=gath.at[p, y], dst_ref=gath.at[p, y],
-            send_sem=agy_s.at[p], recv_sem=agy_r.at[p],
-            device_id={"coil": partner}, device_id_type=MESH,
-        )
-
-    def ag_y_one(p):
-        return pltpu.make_async_remote_copy(
-            src_ref=gath.at[p, y, z], dst_ref=gath.at[p, y, z],
-            send_sem=agy_s.at[p], recv_sem=agy_r.at[p],
+    def ag_y(p, src):
+        return pltpu.make_async_remote_copy(
+            src_ref=gath.at[p, y, src], dst_ref=gath.at[p, y, src],
+            send_sem=agy_s.at[p, src], recv_sem=agy_r.at[p, src],
             device_id={"coil": partner}, device_id_type=MESH,
         )
 
@@ -195,7 +188,7 @@
 
         @pl.when(swapped(p))
         def _():
-            ag_y_one(p).start()
+            ag_y(p, z).start()
 
     for copy in halo_copies():
         copy.start()
@@ -204,7 +197,7 @@
     for s in range(slices):
         cols = slice(s * width, (s + 1) * width)
         plain = jnp.concatenate(
-            [map_ref[pl.ds((b % zs * YS + b // zs) * rows, rows), cols] for b in range(coils)], 0
+            [map_ref[pl.ds((b % zs * YS + b // zs) * rows, rows), s, :] for b in range(coils)], 0
         ).astype(jnp.float32)
         turned = pltpu.roll(plain, half, 1)
         fac_a[:, cols] = jnp.where(first, plain, turned)
@@ -213,15 +206,21 @@
     mask[...] = mask_ref[...].astype(jnp.float32).T
 
     def gather_one(p):
+        @pl.when(straight(p))
+        def _():
+            ag_y(p, z).start()
+
         @pl.when(straight(p) & inner)
         def _():
             wait_opp(p, y)
             for copy in ag_relay(p, y):
                 copy.start()
-
-        @pl.when(swapped(p))
-        def _():
-            ag_y_one(p).wait_recv()
+            for k in range(2):
+                ag_y(p, opp + k).start()
+
+        @pl.when(swapped(p))
+        def _():
+            ag_y(p, z).wait_recv()
             for copy in ag_own(p, other_y):
                 copy.start()
 
@@ -231,9 +230,11 @@
             @pl.when(outer)
             def _():
                 wait_opp(p, y)
+                for k in range(2):
+                    ag_y(p, opp + k).start()
 
             wait_mate(p, y)
-            ag_y(p).start()
+            ag_y(p, mate).start()
 
         @pl.when(swapped(p) & inner)
         def _():
@@ -245,7 +246,8 @@
     def gather_end(p):
         @pl.when(straight(p))
         def _():
-            ag_y(p).wait_recv()
+            for k in range(zs):
+                ag_y(p, k).wait_recv()
 
         @pl.when(swapped(p))
         def _():
@@ -407,13 +409,14 @@
 
         @pl.when(straight(p))
         def _():
-            ag_y(p).wait_send()
+            for k in range(zs):
+                ag_y(p, k).wait_send()
             rs_y(p).wait_send()
 
         @pl.when(swapped(p))
         def _():
             column_sent(other_y)
-            ag_y_one(p).wait_send()
+            ag_y(p, z).wait_send()
             rs_y_one(p).wait_send()
 
 
@@ -432,7 +435,6 @@
     wf = np.concatenate([forward, -forward[:, half:], forward[:, :half]], 1)
     wb = np.concatenate([backward, backward[:, half:], backward[:, :half]], 1)
 
-    maps = coil_maps[0].reshape(total, lanes)
 
     vmem = pltpu.VMEM
     bf16, f32 = jnp.bfloat16, jnp.float32
@@ -462,7 +464,7 @@
             vmem((phases, YS, 2, rows, lanes), bf16),
             vmem((phases, YS, 2, rows, lanes), bf16),
             dma((phases, YS, 4)), dma((phases, YS, zs)),
-            dma((phases,)), dma((phases,)),
+            dma((phases, zs)), dma((phases, zs)),
             dma((phases,)), dma((phases,)),
             dma((phases, YS, 3)), dma((phases, YS, 2)),
             dma((phases, YS)), dma((phases, YS)),
@@ -471,7 +473,7 @@
         compiler_params=pltpu.CompilerParams(
             collective_id=0, has_side_effects=True, vmem_limit_bytes=56 << 20
         ),
-    )(position, maps, kspace_data[0], sample_mask.T, jnp.asarray(rf), jnp.asarray(rb), jnp.asarray(wf), jnp.asarray(wb))
+    )(position, coil_maps[0], kspace_data[0], sample_mask.T, jnp.asarray(rf), jnp.asarray(rb), jnp.asarray(wf), jnp.asarray(wb))
 
 
 def with_halo(block, sides, width):

time: 90 us -> 86.7 us (0.963)
  local copies, waits for them, and re-layouts: 4.07 us -> 2.28 us
  Pallas kernels: 85.7 us -> 84.3 us
    unnamed x2 -> x1, local copies, waits for them, and re-layouts: 4.07 us -> 2.28 us
    pallas_call x1, Pallas kernels: 85.7 us -> 84.3 us  [fused(): pl.pallas_call(functools.partial(kernel, zs, phases, rows, width), out_sh...]
where the time goes in v4:
time: 86.7 us; the launch traced here: 86.6 us
  Pallas kernels  84.3 us (97%)
  local copies, waits for them, and re-layouts  2.28 us (3%)
    pallas_call x1, Pallas kernels, fused(): pl.pallas_call(functools.partial(kernel, zs, phases, rows, width), out_sh...  84.3 us
    unnamed x1, local copies, waits for them, and re-layouts  2.28 us

profile of v4, /device:TPU:0, one launch (start us, length us, event | category | flops | bytes accessed | tf_op | source)
XLA Modules:
  0.0 86.6 jit_solution(18155228004215822248)
XLA Ops:
  0.0 84.3 %shard_map.82 = f32[32,8,2,384]{3,2,1,0:T(2,128)} custom-call(f32[32,8,2,384]{3,2,1,0:T(2,128)} %pos_ref.1, bf16[256,2,384]{2,1,0:T(2,128)(2,1)} %bitcast.4, bf16[256,8,2,384]{3,2,1,0:T(2,128)(2,1)} %bitcast.3, s32[8,256]{1,0:T(8,128)} %bitcast.5, bf16[256,512]{1,0:T(8,128)(2,1)} %constant.8.clone.rf_ref, bf16[256,512]{1,0:T(8,128)(2,1)} %constant.9.clone.rb_ref, ...), custom_call_target="tpu_custom_call" | custom-call | tf_op jit(solution)/shard_map/pallas_call | solution.py:442
  84.3 2.3 %copy.10 = f32[32,8,2,384]{3,2,1,0:T(2,128)} copy(f32[32,8,2,384]{3,2,1,0:T(2,128)} %shard_map.82) | data formatting | bytes 1572864

commit v5 on v4

--- a/solution.py
+++ b/solution.py
@@ -83,8 +83,7 @@
     def data_copy(p):
         return pltpu.make_async_copy(data_hbm.at[:, p], data.at[p], data_s.at[p])
 
-    @pl.loop(0, phases)
-    def _(p):
+    def prepare(p):
         data_copy(p).start()
         for s in range(slices):
             cols = slice(s * width, (s + 1) * width)
@@ -95,6 +94,7 @@
         low[p] = here.astype(jnp.bfloat16)
         gath[p, y, z] = low[p]
 
+    prepare(0)
     pl.semaphore_wait(barrier, len(peers))
 
     def ag_z(p, col, src, to, slot):
@@ -183,6 +183,10 @@
 
     @pl.loop(0, phases)
     def _(p):
+        @pl.when(p > 0)
+        def _():
+            prepare(p)
+
         for copy in ag_own(p, y):
             copy.start()
 

time: 86.7 us -> 86.7 us (level)
  no operation moved by 1% of the time
where the time goes in v5:
time: 86.7 us; the launch traced here: 86.6 us
  Pallas kernels  84.3 us (97%)
  local copies, waits for them, and re-layouts  2.28 us (3%)
    pallas_call x1, Pallas kernels, fused(): pl.pallas_call(functools.partial(kernel, zs, phases, rows, width), out_sh...  84.3 us
    unnamed x1, local copies, waits for them, and re-layouts  2.28 us

profile of v5, /device:TPU:0, one launch (start us, length us, event | category | flops | bytes accessed | tf_op | source)
XLA Modules:
  0.0 86.6 jit_solution(10951272539103647719)
XLA Ops:
  0.0 84.3 %shard_map.82 = f32[32,8,2,384]{3,2,1,0:T(2,128)} custom-call(f32[32,8,2,384]{3,2,1,0:T(2,128)} %pos_ref.1, bf16[256,2,384]{2,1,0:T(2,128)(2,1)} %bitcast.4, bf16[256,8,2,384]{3,2,1,0:T(2,128)(2,1)} %bitcast.3, s32[8,256]{1,0:T(8,128)} %bitcast.5, bf16[256,512]{1,0:T(8,128)(2,1)} %constant.8.clone.rf_ref, bf16[256,512]{1,0:T(8,128)(2,1)} %constant.9.clone.rb_ref, ...), custom_call_target="tpu_custom_call" | custom-call | tf_op jit(solution)/shard_map/pallas_call | solution.py:446
  84.3 2.3 %copy.10 = f32[32,8,2,384]{3,2,1,0:T(2,128)} copy(f32[32,8,2,384]{3,2,1,0:T(2,128)} %shard_map.82) | data formatting | bytes 1572864
